TPU v7x, 256 devices: a whole 4x4x8 slice. The times are simulated.
256 devices in a mesh: tok: 32 (over x, y, core), feat: 8 (over z).
Axes of the slice: x: 4, y: 4, z: 8, core: 2. Of those that a mesh axis runs over, the one named last changes fastest.
Arguments:
- inputs: bfloat16 [16384, 2048], P(('tok', 'feat'))
- norm_gain: float32 [2048], replicated, may hold values from 0.1 to 1.9
- w_in: bfloat16 [512, 8192], P('tok', 'feat'), may hold values from -0.25 to 0.25
- w_out: bfloat16 [512, 8192], P('tok', 'feat'), may hold values from -0.125 to 0.125
- block_index: int32 [64, 4], P('feat'), may hold values from 0 to 15, all different within a row
- segment_ids: int32 [16384], P(('tok', 'feat')), may hold values from 0 to 1023, never falling along the last dimension, each value on 1 to 24 neighbouring positions
- teacher_scores: float32 [1024], replicated, may hold values from -6 to 6
- upstream: bfloat16 [16384, 2048], P(('tok', 'feat')), may hold values from -6 to 6
- readout: float32 [2048], replicated, may hold values from -0.125 to 0.125
Outputs:
- layer_out: bfloat16 [16384, 2048], P(('tok', 'feat'))
- input_grad: bfloat16 [16384, 2048], P(('tok', 'feat'))
- grad_in: float32 [512, 8192], P('tok', 'feat')
- grad_out: float32 [512, 8192], P('tok', 'feat')
Inputs may be any that keep to these rules, and one draw needn't show every extreme that they name: `block_index`: each row names 4 different feature blocks; every feature block is named by some row. `segment_ids`: never falls along the tokens; every segment 0 to 1023 holds 1 to 24 tokens.
All inputs are finite; a program needn't handle non-finite values.
Results may differ from a plain program's by a relative error of at most 0.015.
Values may be sent and summed in bfloat16 or wider, within the bound.
A program may use at most 128 MiB of HBM per device.

v0:
```python
import math
import jax
import jax.numpy as jnp
from jax import lax
from jax.sharding import PartitionSpec as P

BLK = 128
EPS = 1e-06
LOSS_WEIGHT = 8.0


def gelu_tanh(values):
    return jax.nn.gelu(values, approximate=True)


def gelu_back(values, cotangent):
    return jax.vjp(gelu_tanh, values)[1](cotangent)[0]


def on_device(
    inputs, norm_gain, w_in, w_out, block_index, segment_ids, teacher_scores, upstream, readout
):
    local_tokens, model_width = inputs.shape
    blocks_here = w_in.shape[1] // BLK
    feature_blocks = model_width // BLK
    per_hidden = block_index.shape[1]
    total_tokens = local_tokens * lax.axis_size("tok") * lax.axis_size("feat")
    grad_scale = 1.0 / math.sqrt(total_tokens)
    inputs_wide = inputs.astype(jnp.float32)
    mean_square = jnp.mean(inputs_wide * inputs_wide, axis=1, keepdims=True)
    inv_rms = lax.rsqrt(mean_square + EPS)
    normed = (inputs_wide * inv_rms * norm_gain[None, :]).astype(jnp.bfloat16)
    w_in_all, w_out_all = (
        lax.all_gather(w_in, "tok", axis=0, tiled=True),
        lax.all_gather(w_out, "tok", axis=0, tiled=True),
    )
    picked_width = w_in_all.shape[0]
    w_in_blocks = w_in_all.reshape(picked_width, blocks_here, BLK)
    w_out_blocks = w_out_all.reshape(picked_width, blocks_here, BLK)
    normed_rows = lax.all_gather(normed, "feat", axis=0, tiled=True)
    group_rows = normed_rows.shape[0]
    one_hot = block_index[:, :, None] == jnp.arange(feature_blocks, dtype=jnp.int32)[None, None, :]
    sel_half = one_hot.astype(jnp.bfloat16)
    sel_wide = one_hot.astype(jnp.float32)

    def select(rows):
        blocks = rows.reshape(group_rows, feature_blocks, BLK)
        picked = jnp.einsum("rdc,jkd->rjkc", blocks, sel_half, preferred_element_type=jnp.float32)
        return picked.astype(jnp.bfloat16).reshape(group_rows, blocks_here, picked_width)

    def spread(terms):
        grouped = terms.reshape(group_rows, blocks_here, per_hidden, BLK)
        placed = jnp.einsum("rjkc,jkd->rdc", grouped, sel_wide, precision=lax.Precision.HIGHEST)
        return placed.reshape(group_rows, model_width)

    chosen = select(normed_rows)
    pre_act = jnp.einsum("rjm,mjc->rjc", chosen, w_in_blocks, preferred_element_type=jnp.float32)
    activated = gelu_tanh(pre_act).astype(jnp.bfloat16)
    out_terms_fwd = jnp.einsum(
        "rjc,mjc->rjm", activated, w_out_blocks, preferred_element_type=jnp.float32
    )
    branch = lax.psum_scatter(
        spread(out_terms_fwd).astype(jnp.bfloat16), "feat", scatter_dimension=0, tiled=True
    ).astype(jnp.float32)
    layer_out = (inputs_wide + branch).astype(jnp.bfloat16)
    token_score = jnp.dot(layer_out.astype(jnp.float32), readout, precision=lax.Precision.HIGHEST)
    segment_count = teacher_scores.shape[0]
    member = (segment_ids[:, None] == jnp.arange(segment_count, dtype=jnp.int32)[None, :]).astype(
        jnp.float32
    )
    score_sums = jnp.dot(token_score, member, precision=lax.Precision.HIGHEST)
    token_counts = jnp.sum(member, axis=0)
    score_sums, token_counts = lax.psum((score_sums, token_counts), ("tok", "feat"))
    misfit = score_sums / token_counts - teacher_scores
    token_coeff = 2.0 * LOSS_WEIGHT * jnp.sum(member * misfit[None, :], axis=1)
    cotangent_local = (
        upstream.astype(jnp.float32) + token_coeff[:, None] * readout[None, :]
    ).astype(jnp.bfloat16)
    cotangent_rows = lax.all_gather(cotangent_local, "feat", axis=0, tiled=True)
    chosen_grad = select(cotangent_rows)
    upper_grad = jnp.einsum(
        "rjm,mjc->rjc", chosen_grad, w_out_blocks, preferred_element_type=jnp.float32
    )
    pre_grad = gelu_back(pre_act, upper_grad).astype(jnp.bfloat16)

    def arrange(terms):
        return terms.reshape(picked_width, blocks_here * BLK) * grad_scale

    back_terms = jnp.einsum(
        "rjc,mjc->rjm", pre_grad, w_in_blocks, preferred_element_type=jnp.float32
    )
    out_terms = jnp.einsum(
        "rjm,rjc->mjc", chosen_grad, activated, preferred_element_type=jnp.float32
    )
    in_terms = jnp.einsum("rjm,rjc->mjc", chosen, pre_grad, preferred_element_type=jnp.float32)
    grad_out, grad_in = (
        lax.psum_scatter(
            arrange(out_terms).astype(jnp.bfloat16), "tok", scatter_dimension=0, tiled=True
        ).astype(jnp.float32),
        lax.psum_scatter(
            arrange(in_terms).astype(jnp.bfloat16), "tok", scatter_dimension=0, tiled=True
        ).astype(jnp.float32),
    )
    back_sum = lax.psum_scatter(
        spread(back_terms).astype(jnp.bfloat16), "feat", scatter_dimension=0, tiled=True
    ).astype(jnp.float32)
    scaled = back_sum * norm_gain[None, :]
    inner_mean = jnp.mean(scaled * inputs_wide, axis=1, keepdims=True)
    norm_back = inv_rms * scaled - inputs_wide * (inv_rms * inv_rms * inv_rms) * inner_mean
    input_grad = (cotangent_local.astype(jnp.float32) + norm_back).astype(jnp.bfloat16)
    return (layer_out, input_grad, grad_in, grad_out)


def solution(mesh):
    return jax.shard_map(
        on_device,
        mesh=mesh,
        in_specs=(
            P(("tok", "feat"), None),
            P(),
            P("tok", "feat"),
            P("tok", "feat"),
            P("feat", None),
            P(("tok", "feat")),
            P(),
            P(("tok", "feat"), None),
            P(),
        ),
        out_specs=(
            P(("tok", "feat"), None),
            P(("tok", "feat"), None),
            P("tok", "feat"),
            P("tok", "feat"),
        ),
        check_vma=False,
    )
```

profile of v0, /device:TPU:2, one launch (start us, length us, event | category | flops | bytes accessed | tf_op | source)
XLA Modules:
  0.0 581.6 jit_solution(5638336384249948303)
XLA Ops:
  9.8 1.8 fusion.27
  11.7 49.1 %all-gather.7.cloned.1.call-done = bf16[512,1024]{1,0:T(8,128)(2,1)} async-done(((bf16[16,1024]{1,0:T(8,128)(2,1)}), bf16[512,1024]{1,0:T(8,128)(2,1)}) %all-gather.7.cloned.1.call-update) | async-done | bytes 1048592 | tf_op jit(solution)/shard_map/all_gather | solution.py:34
  60.8 1.5 copy.56
  62.3 48.1 %all-gather.9.cloned.1.call-done = bf16[512,1024]{1,0:T(8,128)(2,1)} async-done(((bf16[16,1024]{1,0:T(8,128)(2,1)}), bf16[512,1024]{1,0:T(8,128)(2,1)}) %all-gather.9.cloned.1.call-update) | async-done | bytes 1048592 | tf_op jit(solution)/shard_map/all_gather | solution.py:35
  110.3 1.5 copy.59
  111.8 41.5 %all-gather.5.cloned.1.call-done = bf16[512,2048]{1,0:T(8,128)(2,1)} async-done(((bf16[64,2048]{1,0:T(8,128)(2,1)}), bf16[512,2048]{1,0:T(8,128)(2,1)}) %all-gather.5.cloned.1.call-update) | async-done | bytes 2097168 | tf_op jit(solution)/shard_map/all_gather | solution.py:40
  153.3 2.2 copy.82
  157.6 1.4 fusion.6
  159.5 4.5 fusion.47
  164.1 10.4 %copy.61 = f32[512,8,4,128]{3,1,2,0:T(8,128)} copy(f32[512,8,4,128]{0,3,2,1:T(8,128)} %bitcast.104) | data formatting | bytes 16777216 | tf_op jit(solution)/shard_map/reshape | solution.py:52
  174.5 5.6 bitcast_convert_fusion.1
  180.1 1.9 copy.107
  182.7 40.9 %reduce-scatter.5.cloned.1.call-done = bf16[64,2048]{1,0:T(8,128)(2,1)} async-done(((bf16[512,2048]{1,0:T(8,128)(2,1)}), bf16[64,2048]{1,0:T(8,128)(2,1)}) %reduce-scatter.5.cloned.1.call-update) | async-done | bytes 262160 | tf_op jit(solution)/shard_map/reduce_scatter | solution.py:62
  225.9 74.4 %all-reduce = (f32[1024]{0:T(1024)S(1)}, f32[1024]{0:T(1024)S(1)}) all-reduce(f32[1024]{0:T(1024)S(1)} %bitcast.124, f32[1024]{0:T(1024)S(1)} %convert_reduce_fusion), channel_id=1, replica_groups=mesh['tok'=32,'feat'=8] {'tok','feat'}, use_global_device_ids=true, to_apply=%region_2.0 | all-reduce | flops 2048 | bytes 16384 | tf_op jit(solution)/shard_map/psum | solution.py:73
  301.6 37.5 %all-gather.11.cloned.1.call-done = bf16[512,2048]{1,0:T(8,128)(2,1)} async-done(((bf16[64,2048]{1,0:T(8,128)(2,1)}), bf16[512,2048]{1,0:T(8,128)(2,1)}) %all-gather.11.cloned.1.call-update) | async-done | bytes 2097168 | tf_op jit(solution)/shard_map/all_gather | solution.py:79
  339.1 2.2 copy.84
  341.3 1.3 convert_bitcast_fusion
  344.2 3.7 fusion.14
  347.9 3.6 multiply_convert_fusion.1
  351.5 2.4 copy.69
  354.0 6.2 %multiply_convert_fusion = bf16[8,128,512]{2,1,0:T(8,128)(2,1)} fusion(bf16[512,8,512]{2,1,0:T(8,128)(2,1)} %bitcast.116, f32[8,512,128]{2,1,0:T(8,128)S(1)} %copy-done.6), kind=kOutput, calls=%fused_computation.32 | convolution fusion | flops 542638080 | bytes 7340032 | tf_op jit(solution)/shard_map/rjm,rjc->mjc/dot_general | solution.py:92
  360.2 2.4 copy.72
  362.8 4.5 fusion.49
  367.4 10.5 %copy.66 = f32[512,8,4,128]{3,1,2,0:T(8,128)} copy(f32[512,8,4,128]{0,3,2,1:T(8,128)} %bitcast.103) | data formatting | bytes 16777216 | tf_op jit(solution)/shard_map/reshape | solution.py:52
  377.8 5.6 bitcast_convert_fusion
  383.5 1.9 copy.106
  385.4 52.5 %reduce-scatter.9.cloned.1.call-done = bf16[16,1024]{1,0:T(8,128)(2,1)} async-done(((bf16[512,1024]{1,0:T(8,128)(2,1)}), bf16[16,1024]{1,0:T(8,128)(2,1)}) %reduce-scatter.9.cloned.1.call-update) | async-done | bytes 32784 | tf_op jit(solution)/shard_map/reduce_scatter | solution.py:100
  437.8 1.4 convert_element_type.118
  439.2 87.3 %reduce-scatter.11.cloned.1.call-done = bf16[16,1024]{1,0:T(8,128)(2,1)} async-done(((bf16[512,1024]{1,0:T(8,128)(2,1)}), bf16[16,1024]{1,0:T(8,128)(2,1)}) %reduce-scatter.11.cloned.1.call-update) | async-done | bytes 32784 | tf_op jit(solution)/shard_map/reduce_scatter | solution.py:97
  526.5 1.4 convert_element_type.122
  527.9 43.7 %reduce-scatter.7.cloned.1.call-done = bf16[64,2048]{1,0:T(8,128)(2,1)} async-done(((bf16[512,2048]{1,0:T(8,128)(2,1)}), bf16[64,2048]{1,0:T(8,128)(2,1)}) %reduce-scatter.7.cloned.1.call-update) | async-done | bytes 262160 | tf_op jit(solution)/shard_map/reduce_scatter | solution.py:104
  572.8 2.0 fusion.32
  (65 shorter events, 12.6 us)
Async XLA Ops:
  7.2 53.6 %all-gather.7.cloned.1.call-start = ((), (), s32[]{:S(2)}) async-start(), calls=%async_computation.5 | async-start | bytes 1081344 | tf_op jit(solution)/shard_map/all_gather | solution.py:34
  7.9 102.4 %all-gather.9.cloned.1.call-start = ((), (), s32[]{:S(2)}) async-start(), calls=%async_computation.6 | async-start | bytes 1081344 | tf_op jit(solution)/shard_map/all_gather | solution.py:35
  8.6 144.7 %all-gather.5.cloned.1.call-start = ((), (), s32[]{:S(2)}) async-start(), calls=%async_computation.4 | async-start | bytes 2359296 | tf_op jit(solution)/shard_map/all_gather | solution.py:40
  11.6 212.0 %reduce-scatter.5.cloned.1.call-start = ((), (), s32[]{:S(2)}) async-start(), calls=%async_computation.7 | async-start | bytes 2359296 | tf_op jit(solution)/shard_map/reduce_scatter | solution.py:62
  153.3 2.2 copy-start.12
  157.6 2.0 copy-start.1
  159.5 4.6 copy-start.4
  182.0 0.7 copy-start.16
  182.0 41.6 %copy-start = (bf16[64,2048]{1,0:T(8,128)(2,1)S(1)}, bf16[64,2048]{1,0:T(8,128)(2,1)}, u32[]{:S(2)}) copy-start(bf16[64,2048]{1,0:T(8,128)(2,1)} %param.9) | copy-start | bytes 786436
  182.0 43.4 %copy-start.14 = (f32[2048]{0:T(1024)S(1)}, f32[2048]{0:T(1024)}, u32[]{:S(2)}) copy-start(f32[2048]{0:T(1024)} %param.17) | copy-start | bytes 24580
  182.0 118.3 %copy-start.15 = (f32[1024]{0:T(1024)S(1)}, f32[1024]{0:T(1024)}, u32[]{:S(2)}) copy-start(f32[1024]{0:T(1024)} %param.15) | copy-start | bytes 12292
  182.0 118.5 %copy-start.9 = (bf16[64,2048]{1,0:T(8,128)(2,1)S(1)}, bf16[64,2048]{1,0:T(8,128)(2,1)}, u32[]{:S(2)}) copy-start(bf16[64,2048]{1,0:T(8,128)(2,1)} %param.16) | copy-start | bytes 786436
  182.0 157.0 %all-gather.11.cloned.1.call-start = ((), (), s32[]{:S(2)}) async-start(), calls=%async_computation.8 | async-start | bytes 2359296 | tf_op jit(solution)/shard_map/all_gather | solution.py:79
  224.6 0.7 copy-start.11
  301.4 136.4 %reduce-scatter.9.cloned.1.call-start = ((), (), s32[]{:S(2)}) async-start(), calls=%async_computation.10 | async-start | bytes 1081344 | tf_op jit(solution)/shard_map/reduce_scatter | solution.py:100
  342.6 1.6 copy-start.5
  343.3 4.5 copy-start.3
  344.2 3.7 copy-start.2
  347.9 3.6 copy-start.7
  351.5 2.5 copy-start.6
  353.9 172.6 %reduce-scatter.11.cloned.1.call-start = ((), (), s32[]{:S(2)}) async-start(), calls=%async_computation.11 | async-start | bytes 1081344 | tf_op jit(solution)/shard_map/reduce_scatter | solution.py:97
  360.2 2.7 copy-start.8
  362.6 209.1 %reduce-scatter.7.cloned.1.call-start = ((), (), s32[]{:S(2)}) async-start(), calls=%async_computation.9 | async-start | bytes 2359296 | tf_op jit(solution)/shard_map/reduce_scatter | solution.py:104
  385.3 186.3 %copy-start.13 = (f32[2048]{0:T(1024)S(1)}, f32[2048]{0:T(1024)}, u32[]{:S(2)}) copy-start(f32[2048]{0:T(1024)} %param.10) | copy-start | bytes 24580
  385.4 187.4 %copy-start.10 = (bf16[64,2048]{1,0:T(8,128)(2,1)S(1)}, bf16[64,2048]{1,0:T(8,128)(2,1)}, u32[]{:S(2)}) copy-start(bf16[64,2048]{1,0:T(8,128)(2,1)} %param.16) | copy-start | bytes 786436
Sparse Core Ops, SparseCore 0:
  10.5 50.1 all-gather.6
  63.3 46.9 all-gather.8
  112.7 40.5 all-gather.4
  182.1 41.4 reduce-scatter.4
  301.5 37.5 all-gather.10
  354.1 83.7 reduce-scatter.8
  441.6 84.8 reduce-scatter.10
  529.1 42.5 reduce-scatter.6
where the time goes:
time: 583 us; the launch traced here: 582 us
  waiting for transfers between devices  402 us (69%)
  blocking collectives  74.4 us (13%)
  local copies, waits for them, and re-layouts  41 us (7%)
  matrix products  38.3 us (7%)
  between operations  14.4 us (2%)
  other arithmetic  11 us (2%)
    reduce_scatter x1, waiting for transfers between devices, on_device(): lax.psum_scatter(arrange(out_terms).astype(jnp.bfloat16), 'tok', scatter_...  87.3 us
    psum x1, blocking collectives, on_device(): lax.psum((score_sums, token_counts), ('tok', 'feat'))  74.4 us
    reduce_scatter x1, waiting for transfers between devices, on_device(): lax.psum_scatter(arrange(in_terms).astype(jnp.bfloat16), 'tok', scatter_d...  52.5 us
    all_gather x1, waiting for transfers between devices, on_device(): lax.all_gather(w_in, 'tok', axis=0, tiled=True)  49.1 us
    all_gather x1, waiting for transfers between devices, on_device(): lax.all_gather(w_out, 'tok', axis=0, tiled=True)  48.1 us
    reduce_scatter x1, waiting for transfers between devices, on_device(): lax.psum_scatter(spread(back_terms).astype(jnp.bfloat16), 'feat', scatter...  43.7 us
    all_gather x1, waiting for transfers between devices, on_device(): normed_rows = lax.all_gather(normed, 'feat', axis=0, tiled=True)  41.5 us
    reduce_scatter x1, waiting for transfers between devices, on_device(): lax.psum_scatter(spread(out_terms_fwd).astype(jnp.bfloat16), 'feat', scat...  40.9 us
  transfers between devices with their start and end apart: 8, of which 8 were waited for; matrix products, arithmetic and copies ran while one was open for 7% of the time, Pallas kernels for 0%

commit v1 on v0

--- a/solution.py
+++ b/solution.py
@@ -20,6 +20,19 @@
 def on_device(
     inputs, norm_gain, w_in, w_out, block_index, segment_ids, teacher_scores, upstream, readout
 ):
+
+    def sample_track(slab_in):
+        y = jnp.concatenate(
+            lax.all_to_all(
+                jnp.stack([slab_in for _ in range(lax.axis_size("tok"))], axis=0),
+                "tok",
+                split_axis=0,
+                concat_axis=0,
+            ),
+            axis=0,
+        )
+        return y
+
     local_tokens, model_width = inputs.shape
     blocks_here = w_in.shape[1] // BLK
     feature_blocks = model_width // BLK
@@ -30,10 +43,7 @@
     mean_square = jnp.mean(inputs_wide * inputs_wide, axis=1, keepdims=True)
     inv_rms = lax.rsqrt(mean_square + EPS)
     normed = (inputs_wide * inv_rms * norm_gain[None, :]).astype(jnp.bfloat16)
-    w_in_all, w_out_all = (
-        lax.all_gather(w_in, "tok", axis=0, tiled=True),
-        lax.all_gather(w_out, "tok", axis=0, tiled=True),
-    )
+    w_in_all, w_out_all = (lax.all_gather(w_in, "tok", axis=0, tiled=True), sample_track(w_out))
     picked_width = w_in_all.shape[0]
     w_in_blocks = w_in_all.reshape(picked_width, blocks_here, BLK)
     w_out_blocks = w_out_all.reshape(picked_width, blocks_here, BLK)

time: 583 us -> 536 us (0.919)
  waiting for transfers between devices: 402 us -> 334 us
  blocking collectives: 74.4 us -> 96.6 us
    all_gather x1 -> x0, waiting for transfers between devices: 48.1 us -> none  [on_device(): lax.all_gather(w_out, 'tok', axis=0, tiled=True)]
    all_to_all x0 -> x1, blocking collectives: none -> 22.1 us  [sample_track(): lax.all_to_all(jnp.stack([slab_in for _ in range(lax.axis_size('tok'))],...]
    all_gather x1, waiting for transfers between devices: 49.1 us -> 29.7 us  [on_device(): lax.all_gather(w_in, 'tok', axis=0, tiled=True)]
  transfers between devices with their start and end apart: 8 -> 7, of which waited for: 8 -> 7; matrix products, arithmetic and copies ran while one was open for 7% -> 7% of each run, Pallas kernels for 0% -> 0%
where the time goes in v1:
time: 536 us; the launch traced here: 535 us
  waiting for transfers between devices  334 us (62%)
  blocking collectives  96.6 us (18%)
  local copies, waits for them, and re-layouts  40.6 us (8%)
  matrix products  38.4 us (7%)
  between operations  14.4 us (3%)
  other arithmetic  11 us (2%)
    reduce_scatter x1, waiting for transfers between devices, on_device(): lax.psum_scatter(arrange(out_terms).astype(jnp.bfloat16), 'tok', scatter_...  87.2 us
    psum x1, blocking collectives, on_device(): lax.psum((score_sums, token_counts), ('tok', 'feat'))  74.5 us
    reduce_scatter x1, waiting for transfers between devices, on_device(): lax.psum_scatter(arrange(in_terms).astype(jnp.bfloat16), 'tok', scatter_d...  52.5 us
    reduce_scatter x1, waiting for transfers between devices, on_device(): lax.psum_scatter(spread(back_terms).astype(jnp.bfloat16), 'feat', scatter...  43.7 us
    all_gather x1, waiting for transfers between devices, on_device(): normed_rows = lax.all_gather(normed, 'feat', axis=0, tiled=True)  41.5 us
    reduce_scatter x1, waiting for transfers between devices, on_device(): lax.psum_scatter(spread(out_terms_fwd).astype(jnp.bfloat16), 'feat', scat...  40.8 us
    all_gather x1, waiting for transfers between devices, on_device(): cotangent_rows = lax.all_gather(cotangent_local, 'feat', axis=0, tiled=True)  37.5 us
    all_gather x1, waiting for transfers between devices, on_device(): lax.all_gather(w_in, 'tok', axis=0, tiled=True)  29.7 us
  transfers between devices with their start and end apart: 7, of which 7 were waited for; matrix products, arithmetic and copies ran while one was open for 7% of the time, Pallas kernels for 0%

profile of v1, /device:TPU:2, one launch (start us, length us, event | category | flops | bytes accessed | tf_op | source)
XLA Modules:
  0.0 535.2 jit_solution(5882639989818358755)
XLA Ops:
  9.1 1.8 fusion.30
  11.8 22.1 %all_to_all.5 = bf16[32,16,1024]{2,1,0:T(8,128)(2,1)S(1)} all-to-all(bf16[32,16,1024]{2,1,0:T(8,128)(2,1)S(1)} %stack.2), channel_id=1, replica_groups=mesh['tok'=32,'feat'=8] {'tok'}, dimensions={0} | all-to-all | bytes 2097152 | tf_op jit(solution)/shard_map/all_to_all | solution.py:26
  34.1 29.7 %all-gather.6.cloned.1.call-done = bf16[512,1024]{1,0:T(8,128)(2,1)} async-done(((bf16[16,1024]{1,0:T(8,128)(2,1)}), bf16[512,1024]{1,0:T(8,128)(2,1)}) %all-gather.6.cloned.1.call-update) | async-done | bytes 1048592 | tf_op jit(solution)/shard_map/all_gather | solution.py:46
  63.9 1.5 copy.54
  65.4 41.5 %all-gather.4.cloned.1.call-done = bf16[512,2048]{1,0:T(8,128)(2,1)} async-done(((bf16[64,2048]{1,0:T(8,128)(2,1)}), bf16[512,2048]{1,0:T(8,128)(2,1)}) %all-gather.4.cloned.1.call-update) | async-done | bytes 2097168 | tf_op jit(solution)/shard_map/all_gather | solution.py:50
  106.9 2.2 copy.77
  109.1 1.3 convert_bitcast_fusion.1
  111.1 1.4 fusion.6
  113.0 4.6 fusion.26
  117.6 10.4 %copy.58 = f32[512,8,4,128]{3,1,2,0:T(8,128)} copy(f32[512,8,4,128]{0,3,2,1:T(8,128)} %bitcast.104) | data formatting | bytes 16777216 | tf_op jit(solution)/shard_map/reshape | solution.py:62
  128.0 5.6 %bitcast_convert_fusion.1 = bf16[16,512,128]{2,0,1:T(8,128)(2,1)S(1)} fusion(f32[512,8,4,128]{3,1,2,0:T(8,128)} %copy.58, s32[8,4]{0,1:T(4,128)S(1)} %copy-done.12), kind=kOutput, calls=%fused_computation.1 | convolution fusion | flops 403702272 | bytes 10485888 | tf_op jit(solution)/shard_map/rjkc,jkd->rdc/dot_general | solution.py:63
  133.6 1.9 copy.107
  136.3 40.8 %reduce-scatter.5.cloned.1.call-done = bf16[64,2048]{1,0:T(8,128)(2,1)} async-done(((bf16[512,2048]{1,0:T(8,128)(2,1)}), bf16[64,2048]{1,0:T(8,128)(2,1)}) %reduce-scatter.5.cloned.1.call-update) | async-done | bytes 262160 | tf_op jit(solution)/shard_map/reduce_scatter | solution.py:72
  179.4 74.5 %all-reduce = (f32[1024]{0:T(1024)S(1)}, f32[1024]{0:T(1024)S(1)}) all-reduce(f32[1024]{0:T(1024)S(1)} %bitcast.125, f32[1024]{0:T(1024)S(1)} %convert_reduce_fusion), channel_id=1, replica_groups=mesh['tok'=32,'feat'=8] {'tok','feat'}, use_global_device_ids=true, to_apply=%region_2.0 | all-reduce | flops 2048 | bytes 16384 | tf_op jit(solution)/shard_map/psum | solution.py:83
  255.2 37.5 %all-gather.8.cloned.1.call-done = bf16[512,2048]{1,0:T(8,128)(2,1)} async-done(((bf16[64,2048]{1,0:T(8,128)(2,1)}), bf16[512,2048]{1,0:T(8,128)(2,1)}) %all-gather.8.cloned.1.call-update) | async-done | bytes 2097168 | tf_op jit(solution)/shard_map/all_gather | solution.py:89
  292.7 2.2 copy.80
  294.9 1.3 convert_bitcast_fusion
  297.8 3.8 fusion.14
  301.6 3.6 multiply_convert_fusion.1
  305.2 2.4 copy.66
  307.7 6.1 %multiply_convert_fusion = bf16[8,128,512]{2,1,0:T(8,128)(2,1)} fusion(bf16[512,8,512]{2,1,0:T(8,128)(2,1)} %bitcast.116, f32[8,512,128]{2,1,0:T(8,128)S(1)} %copy-done.6), kind=kOutput, calls=%fused_computation.32 | convolution fusion | flops 542638080 | bytes 7340032 | tf_op jit(solution)/shard_map/rjm,rjc->mjc/dot_general | solution.py:102
  313.9 2.4 copy.69
  316.5 4.5 fusion.51
  321.1 10.5 %copy.63 = f32[512,8,4,128]{3,1,2,0:T(8,128)} copy(f32[512,8,4,128]{0,3,2,1:T(8,128)} %bitcast.103) | data formatting | bytes 16777216 | tf_op jit(solution)/shard_map/reshape | solution.py:62
  331.5 5.6 %bitcast_convert_fusion = bf16[16,512,128]{2,0,1:T(8,128)(2,1)S(1)} fusion(f32[512,8,4,128]{3,1,2,0:T(8,128)} %copy.63, s32[8,4]{0,1:T(4,128)S(1)} %copy-done.12), kind=kOutput, calls=%fused_computation | convolution fusion | flops 403702272 | bytes 10485888 | tf_op jit(solution)/shard_map/rjkc,jkd->rdc/dot_general | solution.py:63
  337.2 1.9 copy.106
  339.1 52.5 %reduce-scatter.9.cloned.1.call-done = bf16[16,1024]{1,0:T(8,128)(2,1)} async-done(((bf16[512,1024]{1,0:T(8,128)(2,1)}), bf16[16,1024]{1,0:T(8,128)(2,1)}) %reduce-scatter.9.cloned.1.call-update) | async-done | bytes 32784 | tf_op jit(solution)/shard_map/reduce_scatter | solution.py:110
  391.6 1.4 convert_element_type.118
  393.0 87.2 %reduce-scatter.11.cloned.1.call-done = bf16[16,1024]{1,0:T(8,128)(2,1)} async-done(((bf16[512,1024]{1,0:T(8,128)(2,1)}), bf16[16,1024]{1,0:T(8,128)(2,1)}) %reduce-scatter.11.cloned.1.call-update) | async-done | bytes 32784 | tf_op jit(solution)/shard_map/reduce_scatter | solution.py:107
  480.1 1.4 convert_element_type.122
  481.5 43.7 %reduce-scatter.7.cloned.1.call-done = bf16[64,2048]{1,0:T(8,128)(2,1)} async-done(((bf16[512,2048]{1,0:T(8,128)(2,1)}), bf16[64,2048]{1,0:T(8,128)(2,1)}) %reduce-scatter.7.cloned.1.call-update) | async-done | bytes 262160 | tf_op jit(solution)/shard_map/reduce_scatter | solution.py:114
  526.4 2.0 fusion.35
  (64 shorter events, 11.7 us)
Async XLA Ops:
  7.2 56.7 %all-gather.6.cloned.1.call-start = ((), (), s32[]{:S(2)}) async-start(), calls=%async_computation.6 | async-start | bytes 1081344 | tf_op jit(solution)/shard_map/all_gather | solution.py:46
  7.9 99.0 %all-gather.4.cloned.1.call-start = ((), (), s32[]{:S(2)}) async-start(), calls=%async_computation.5 | async-start | bytes 2359296 | tf_op jit(solution)/shard_map/all_gather | solution.py:50
  10.9 166.2 %reduce-scatter.5.cloned.1.call-start = ((), (), s32[]{:S(2)}) async-start(), calls=%async_computation.7 | async-start | bytes 2359296 | tf_op jit(solution)/shard_map/reduce_scatter | solution.py:72
  106.9 2.2 copy-start.12
  111.1 1.9 copy-start.1
  113.0 4.6 copy-start.4
  135.5 0.7 copy-start.16
  135.5 41.6 %copy-start = (bf16[64,2048]{1,0:T(8,128)(2,1)S(1)}, bf16[64,2048]{1,0:T(8,128)(2,1)}, u32[]{:S(2)}) copy-start(bf16[64,2048]{1,0:T(8,128)(2,1)} %param.9) | copy-start | bytes 786436
  135.5 43.3 %copy-start.14 = (f32[2048]{0:T(1024)S(1)}, f32[2048]{0:T(1024)}, u32[]{:S(2)}) copy-start(f32[2048]{0:T(1024)} %param.17) | copy-start | bytes 24580
  135.5 118.4 %copy-start.15 = (f32[1024]{0:T(1024)S(1)}, f32[1024]{0:T(1024)}, u32[]{:S(2)}) copy-start(f32[1024]{0:T(1024)} %param.15) | copy-start | bytes 12292
  135.5 118.6 %copy-start.9 = (bf16[64,2048]{1,0:T(8,128)(2,1)S(1)}, bf16[64,2048]{1,0:T(8,128)(2,1)}, u32[]{:S(2)}) copy-start(bf16[64,2048]{1,0:T(8,128)(2,1)} %param.16) | copy-start | bytes 786436
  135.5 157.1 %all-gather.8.cloned.1.call-start = ((), (), s32[]{:S(2)}) async-start(), calls=%async_computation.8 | async-start | bytes 2359296 | tf_op jit(solution)/shard_map/all_gather | solution.py:89
  178.1 0.7 copy-start.11
  255.0 136.6 %reduce-scatter.9.cloned.1.call-start = ((), (), s32[]{:S(2)}) async-start(), calls=%async_computation.10 | async-start | bytes 1081344 | tf_op jit(solution)/shard_map/reduce_scatter | solution.py:110
  296.2 1.6 copy-start.5
  296.9 4.7 copy-start.3
  297.8 3.8 copy-start.2
  301.6 3.6 copy-start.7
  305.2 2.5 copy-start.6
  307.7 172.4 %reduce-scatter.11.cloned.1.call-start = ((), (), s32[]{:S(2)}) async-start(), calls=%async_computation.11 | async-start | bytes 1081344 | tf_op jit(solution)/shard_map/reduce_scatter | solution.py:107
  313.9 2.6 copy-start.8
  316.3 209.0 %reduce-scatter.7.cloned.1.call-start = ((), (), s32[]{:S(2)}) async-start(), calls=%async_computation.9 | async-start | bytes 2359296 | tf_op jit(solution)/shard_map/reduce_scatter | solution.py:114
  339.0 186.2 %copy-start.13 = (f32[2048]{0:T(1024)S(1)}, f32[2048]{0:T(1024)}, u32[]{:S(2)}) copy-start(f32[2048]{0:T(1024)} %param.10) | copy-start | bytes 24580
  339.0 187.4 %copy-start.10 = (bf16[64,2048]{1,0:T(8,128)(2,1)S(1)}, bf16[64,2048]{1,0:T(8,128)(2,1)}, u32[]{:S(2)}) copy-start(bf16[64,2048]{1,0:T(8,128)(2,1)} %param.16) | copy-start | bytes 786436
Sparse Core Ops, SparseCore 0:
  10.5 53.2 all-gather.5
  66.2 40.5 all-gather.3
  135.7 41.3 reduce-scatter.4
  255.1 37.5 all-gather.7
  307.8 83.7 reduce-scatter.8
  395.2 84.8 reduce-scatter.10
  482.7 42.5 reduce-scatter.6
